TPU v7x, 256 devices: a whole 4x4x8 slice. The times are simulated.
256 devices in a mesh: brick: 8 (over x_lo, y), bulk: 32 (over x_hi, z, core).
Axes of the slice: x: 4 (x_hi: 2, x_lo: 2; x = x_hi * 2 + x_lo), y: 4, z: 8, core: 2. Of those that a mesh axis runs over, the one named last changes fastest.
Arguments:
- amp_traces: float32 [128, 2048, 256], P(None, ('bulk', 'brick')), may hold values from -6 to 6
- patch_owner: int32 [524288, 1], P(('brick', 'bulk')), may hold values from 0 to 31; in each aligned block of 2048 rows (0 to 2047, 2048 to 4095, ...) at most 256 rows name the same one
- patch_fault: int32 [524288], P(('brick', 'bulk')), may hold values from 0 to 15
- patch_trace: int32 [524288], P(('brick', 'bulk')), may hold values from 0 to 1023
- patch_offset: int32 [524288], P(('brick', 'bulk')), may hold values from 0 to 128
Outputs:
- fault_attr: float32 [128, 2048, 256], P('brick', 'bulk')
- fault_profile: float32 [4096, 128], P(('brick', 'bulk'))
Inputs may be any that keep to these rules, and one draw needn't show every extreme that they name: `patch_owner`: among the 2048 patches of one device, at most 256 name the same owner, and in every draw some device has exactly 256 patches with one owner.
All inputs are finite; a program needn't handle non-finite values.
Results may differ from a plain program's by a relative error of at most 0.0003.
Values sent between devices are 32-bit elements; how exact they have to be, the bound alone decides.
A program may use at most 64 MiB of HBM per device.

v0:
```python
import jax
import jax.numpy as jnp
from jax import lax
from jax.sharding import PartitionSpec as P

PATCH = 128
F_DEV = 16


def padded_2(block, sides, width):
    for axis, dim in sides:
        count = lax.axis_size(axis)
        forward = [(i, i + 1) for i in range(count - 1)]
        backward = [(target, source) for source, target in forward]
        low = lax.ppermute(
            lax.slice_in_dim(block, block.shape[dim] - width, None, axis=dim), axis, forward
        )
        high = lax.ppermute(lax.slice_in_dim(block, 0, width, axis=dim), axis, backward)
        block = jnp.concatenate([low, block, high], axis=dim)
    return block


def box_sum(values, radius, dimension):
    length = values.shape[dimension] - 2 * radius
    summed = lax.slice_in_dim(values, 0, length, axis=dimension)
    for offset in range(1, 2 * radius + 1):
        summed = summed + lax.slice_in_dim(values, offset, offset + length, axis=dimension)
    return summed


def time_sum(values, radius):
    widths = [(0, 0)] * (values.ndim - 1) + [(radius, radius)]
    return box_sum(jnp.pad(values, widths), radius, values.ndim - 1)


def gradient_energy(padded):
    slope_inline = 0.5 * (padded[2:, 1:-1, :] - padded[:-2, 1:-1, :])
    slope_cross = 0.5 * (padded[1:-1, 2:, :] - padded[1:-1, :-2, :])
    centre = jnp.pad(padded[1:-1, 1:-1, :], ((0, 0), (0, 0), (1, 1)))
    slope_time = 0.5 * (centre[:, :, 2:] - centre[:, :, :-2])
    return jnp.stack(
        [slope_inline * slope_inline, slope_cross * slope_cross, slope_time * slope_time]
    )


def smooth_tensor(energy):
    return time_sum(box_sum(box_sum(energy, 2, 1), 2, 2), 2)


def finish(tensor, near_amp):
    lateral = (tensor[0] + tensor[1]) / (tensor[0] + tensor[1] + tensor[2] + 1e-05)
    stack = box_sum(box_sum(near_amp, 1, 0), 1, 1)
    power = box_sum(box_sum(near_amp * near_amp, 1, 0), 1, 1)
    semblance = time_sum(stack * stack, 4) / (9.0 * time_sum(power, 4) + 1e-05)
    return (1.0 - semblance) * lateral


def window_rows(chosen, offsets, width):
    samples = chosen.shape[1]
    steps = (samples - width).bit_length()
    current = chosen
    for level in range(steps):
        amount = 1 << level
        moved = jnp.concatenate(
            [current[:, amount:], jnp.zeros((current.shape[0], amount), current.dtype)], axis=1
        )
        taken = (offsets >> level & 1)[:, None] == 1
        current = jnp.where(taken, moved, current)
    return current[:, :width]


def local(amp_traces, patch_owner, patch_fault, patch_trace, patch_offset):
    bricked = lax.all_to_all(amp_traces, "brick", split_axis=0, concat_axis=1, tiled=True)
    near_amp = padded_2(bricked, (("brick", 0), ("bulk", 1)), 1)
    energy = gradient_energy(near_amp)
    rimmed = padded_2(energy, (("brick", 1), ("bulk", 2)), 2)
    attribute = finish(smooth_tensor(rimmed), near_amp)
    flattened = attribute.reshape(-1, attribute.shape[2])
    chosen = flattened[patch_trace]
    patch_rows = window_rows(chosen, patch_offset, PATCH)
    owners = patch_owner[:, 0]
    owner_count = lax.axis_size("bulk")
    count_patches = patch_rows.shape[0]
    one_hot = (owners[:, None] == jnp.arange(owner_count, dtype=jnp.int32)[None, :]).astype(
        jnp.int32
    )
    placed = jnp.cumsum(one_hot, axis=0)
    slot_rank = jnp.sum(placed * one_hot, axis=1) - 1
    capacity = 4 * count_patches // owner_count
    buffer = (
        jnp.zeros((owner_count, capacity, PATCH), jnp.float32).at[owners, slot_rank].set(patch_rows)
    )
    labels = (
        jnp.zeros((owner_count, capacity), jnp.float32)
        .at[owners, slot_rank]
        .set(patch_fault.astype(jnp.float32) + 1.0)
    )
    got_rows, got_labels = (
        lax.all_to_all(buffer, "bulk", split_axis=0, concat_axis=0, tiled=True),
        lax.all_to_all(labels, "bulk", split_axis=0, concat_axis=0, tiled=True),
    )
    wanted = jnp.arange(F_DEV, dtype=jnp.float32) + 1.0
    selector = (got_labels.reshape(1, -1) == wanted[:, None]).astype(jnp.float32)
    summed = jnp.dot(
        selector,
        got_rows.reshape(-1, PATCH),
        precision=lax.Precision.HIGHEST,
        preferred_element_type=jnp.float32,
    )
    counts = jnp.sum(selector, axis=1)
    profile = summed / jnp.maximum(counts, 1.0)[:, None]
    return (attribute, profile)


def solution(mesh):
    in_specs = (
        P(None, ("bulk", "brick"), None),
        P(("brick", "bulk"), None),
        P(("brick", "bulk")),
        P(("brick", "bulk")),
        P(("brick", "bulk")),
    )
    out_specs = (P("brick", "bulk", None), P(("brick", "bulk"), None))
    return jax.shard_map(local, mesh=mesh, in_specs=in_specs, out_specs=out_specs, check_vma=False)
```

profile of v0, /device:TPU:24, one launch (start us, length us, event | category | flops | bytes accessed | tf_op | source)
XLA Modules:
  0.0 232.0 jit_solution(7785057367832346467)
XLA Ops:
  0.6 0.0 copy-start.6
  0.6 0.0 copy-start.5
  0.7 5.8 %all-to-all-start = ((f32[128,8,256]{2,1,0:T(8,128)}), f32[128,8,256]{2,1,0:T(8,128)S(1)}, u32[]{:S(2)}, u32[]{:S(2)}) async-start(f32[128,8,256]{2,1,0:T(8,128)} %param.5), calls=%async_computation | async-start | bytes 2097152 | tf_op jit(solution)/shard_map/all_to_all | solution.py:73
  6.5 9.1 %reduce-window.6 = s32[32,16,128]{2,1,0:T(8,128)S(1)} reduce-window(s32[32,16,128]{2,1,0:T(8,128)S(1)} %fusion.51, s32[]{:T(128)} %constant.22.clone.1), window={size=1x1x128 pad=0_0x0_0x127_0}, to_apply=%region_0.1 | reduce-window | flops 8323072 | bytes 524292 | tf_op jit(solution)/shard_map/reduce-window
  15.5 0.1 slice.326
  15.7 0.2 copy.14
  15.9 0.2 reduce-window.9
  16.1 0.1 broadcast_add_fusion
  16.3 0.0 copy-start.4
  16.3 0.1 fusion.48
  16.4 0.1 multiply_reduce_fusion
  16.5 0.1 and_reduce_fusion
  16.7 8.6 %scatter_custom_fusion = f32[8192]{0:T(1024)} fusion(s32[2048]{0:T(1024)S(1)} %broadcast_select_fusion, f32[2048]{0:T(1024)S(1)} %convert_add_fusion, f32[]{:T(128)} %constant.18.clone.1), kind=kCustom, calls=%fused_computation.139 | custom fusion | bytes 32772
  25.3 0.0 all-to-all-done
  25.3 11.0 %all-to-all-start.1 = ((f32[32,1,256]{2,1,0:T(1,128)}), f32[32,1,256]{2,1,0:T(1,128)S(1)}, u32[]{:S(2)}, u32[]{:S(2)}) async-start(f32[32,1,256]{2,1,0:T(1,128)} %bitcast.18), calls=%async_computation.1 | async-start | bytes 65536 | tf_op jit(solution)/shard_map/all_to_all | solution.py:100
  36.3 0.1 copy.19
  36.5 2.8 %collective-permute-start = (f32[1,64,256]{2,1,0:T(8,128)S(1)}, f32[1,64,256]{2,1,0:T(8,128)S(1)}, u32[]{:S(2)}, u32[]{:S(2)}) collective-permute-start(f32[1,64,256]{2,1,0:T(8,128)S(1)} %get-tuple-element.13), channel_id=1, source_target_pairs={{0,32},{32,64},{64,96},{96,128},{128,160},{160,192},{192,224},{1,3... | collective-permute-start | bytes 196616 | tf_op jit(solution)/shard_map/ppermute | solution.py:15
  39.2 3.1 %collective-permute-start.1 = (f32[1,64,256]{2,1,0:T(8,128)S(1)}, f32[1,64,256]{2,1,0:T(8,128)S(1)}, u32[]{:S(2)}, u32[]{:S(2)}) collective-permute-start(f32[1,64,256]{2,1,0:T(8,128)S(1)} %get-tuple-element.14), channel_id=1, source_target_pairs={{32,0},{64,32},{96,64},{128,96},{160,128},{192,160},{224,192},{33,... | collective-permute-start | bytes 196616 | tf_op jit(solution)/shard_map/ppermute | solution.py:18
  42.3 0.3 collective-permute-done
  42.6 4.9 %collective-permute-done.1 = f32[1,64,256]{2,1,0:T(8,128)S(1)} collective-permute-done((f32[1,64,256]{2,1,0:T(8,128)S(1)}, f32[1,64,256]{2,1,0:T(8,128)S(1)}, u32[]{:S(2)}, u32[]{:S(2)}) %collective-permute-start.1) | collective-permute-done | bytes 65568 | tf_op jit(solution)/shard_map/ppermute | solution.py:18
  47.5 1.3 collective-permute-start.2
  48.8 1.3 collective-permute-start.3
  50.2 3.8 %collective-permute-done.3 = f32[18,1,256]{2,1,0:T(1,128)S(1)} collective-permute-done((f32[18,1,256]{2,1,0:T(1,128)S(1)}, f32[18,1,256]{2,1,0:T(1,128)S(1)}, u32[]{:S(2)}, u32[]{:S(2)}) %collective-permute-start.3) | collective-permute-done | bytes 18464 | tf_op jit(solution)/shard_map/ppermute | solution.py:18
  53.9 0.9 fusion.42
  54.9 0.1 pad_maximum_fusion.12
  54.9 1.9 collective-permute-start.4
  56.8 3.9 %collective-permute-start.5 = (f32[3,2,64,256]{3,2,1,0:T(8,128)S(1)}, f32[3,2,64,256]{3,2,1,0:T(8,128)S(1)}, u32[]{:S(2)}, u32[]{:S(2)}) collective-permute-start(f32[3,2,64,256]{3,2,1,0:T(8,128)S(1)} %get-tuple-element.5), channel_id=1, source_target_pairs={{32,0},{64,32},{96,64},{128,96},{160,128},{192,160},{224,192},{33,... | collective-permute-start | bytes 1179656 | tf_op jit(solution)/shard_map/ppermute | solution.py:18
  60.8 0.2 pad_maximum_fusion.1
  61.0 0.2 slice_add_fusion.8
  61.2 0.2 fusion.43
  61.4 5.9 %collective-permute-done.4 = f32[3,2,64,256]{3,2,1,0:T(8,128)S(1)} collective-permute-done((f32[3,2,64,256]{3,2,1,0:T(8,128)S(1)}, f32[3,2,64,256]{3,2,1,0:T(8,128)S(1)}, u32[]{:S(2)}, u32[]{:S(2)}) %collective-permute-start.4) | collective-permute-done | bytes 393248 | tf_op jit(solution)/shard_map/ppermute | solution.py:15
  67.3 4.0 %collective-permute-done.5 = f32[3,2,64,256]{3,2,1,0:T(8,128)S(1)} collective-permute-done((f32[3,2,64,256]{3,2,1,0:T(8,128)S(1)}, f32[3,2,64,256]{3,2,1,0:T(8,128)S(1)}, u32[]{:S(2)}, u32[]{:S(2)}) %collective-permute-start.5) | collective-permute-done | bytes 393248 | tf_op jit(solution)/shard_map/ppermute | solution.py:18
  71.3 0.1 pad_maximum_fusion.17
  71.4 3.3 %collective-permute-start.6 = (f32[3,20,2,256]{3,2,1,0:T(2,128)S(1)}, f32[3,20,2,256]{3,2,1,0:T(2,128)S(1)}, u32[]{:S(2)}, u32[]{:S(2)}) collective-permute-start(f32[3,20,2,256]{3,2,1,0:T(2,128)S(1)} %get-tuple-element.2), channel_id=1, source_target_pairs={{0,1},{1,2},{2,3},{3,4},{4,5},{5,6},{6,7},{7,8},{8,9},{9,10},{10,1... | collective-permute-start | bytes 368648 | tf_op jit(solution)/shard_map/ppermute | solution.py:15
  74.7 1.5 collective-permute-start.7
  76.1 0.2 slice_add_fusion.13
  76.4 3.1 %collective-permute-done.7 = f32[3,20,2,256]{3,2,1,0:T(2,128)S(1)} collective-permute-done((f32[3,20,2,256]{3,2,1,0:T(2,128)S(1)}, f32[3,20,2,256]{3,2,1,0:T(2,128)S(1)}, u32[]{:S(2)}, u32[]{:S(2)}) %collective-permute-start.7) | collective-permute-done | bytes 122912 | tf_op jit(solution)/shard_map/ppermute | solution.py:18
  79.5 0.9 pad_maximum_fusion
  80.4 0.5 slice_add_fusion
  80.9 1.2 slice_add_fusion.4
  82.1 4.9 %fusion.3 = f32[3,16,64,256]{3,2,1,0:T(8,128)} fusion(f32[3,16,64,256]{3,2,1,0:T(8,128)S(1)} %slice_add_fusion.4), kind=kLoop, calls=%fused_computation.15 | loop fusion | flops 3145728 | bytes 6291456 | tf_op jit(solution)/shard_map/add | solution.py:27
  87.1 5.9 %fusion.33 = f32[16,64,256]{2,1,0:T(8,128)S(1)} fusion(f32[3,16,64,256]{3,2,1,0:T(8,128)} %fusion.3, f32[16,64,256]{2,1,0:T(8,128)S(1)} %slice_add_fusion.13, f32[16,64,256]{2,1,0:T(8,128)S(1)} %fusion.43), kind=kLoop, calls=%fused_computation.82 | loop fusion | flops 6553600 | bytes 6291456 | tf_op jit(solution)/shard_map/mul | solution.py:55
  92.9 0.0 copy-start
  92.9 6.6 %gather_fusion = f32[2048,256]{1,0:T(8,128)S(1)} fusion(f32[1024,256]{1,0:T(8,128)S(1)} %bitcast.57, s32[2048]{0:T(1024)S(1)} %fusion.54), kind=kCustom, calls=%fused_computation | custom fusion | bytes 4202496 | tf_op jit(solution)/shard_map/gather | solution.py:79
  99.6 0.6 slice.328
  100.2 0.5 pad_select_fusion.6
  100.7 0.6 slice.329
  101.3 0.4 pad_select_fusion.5
  101.8 0.6 slice.330
  102.4 0.4 pad_select_fusion.4
  102.8 0.6 slice.331
  103.4 0.4 pad_select_fusion.3
  103.9 0.6 slice.332
  104.5 0.7 pad_select_fusion.2
  105.2 0.6 slice.333
  105.8 0.4 pad_select_fusion.1
  106.2 0.6 slice.334
  106.8 0.4 pad_select_fusion
  107.3 0.1 slice.335
  107.4 8.9 %scatter_custom_fusion.1 = f32[8192,128]{1,0:T(8,128)} fusion(s32[2048]{0:T(1024)S(1)} %broadcast_select_fusion, f32[]{:T(128)} %constant.18.clone.1, f32[2048,256]{1,0:T(8,128)S(1)} %pad_select_fusion, f32[2048,128]{1,0:T(8,128)S(1)} %slice.335, pred[2048]{0:T(1024)(128)(4,1)S(1)} %get-tuple-element.17), kind=kCustom, calls=%fused_computation.36 | custom fusion | flops 262144 | bytes 6294528
  116.3 14.7 %all-to-all-start.2 = ((f32[32,256,128]{2,1,0:T(8,128)}), f32[32,256,128]{2,1,0:T(8,128)}, u32[]{:S(2)}, u32[]{:S(2)}) async-start(f32[32,256,128]{2,1,0:T(8,128)} %bitcast.62), calls=%async_computation.2 | async-start | bytes 8388608 | tf_op jit(solution)/shard_map/all_to_all | solution.py:99
  131.0 0.3 fusion.45
  131.3 96.4 %all-to-all-done.2 = f32[32,256,128]{2,1,0:T(8,128)} async-done(((f32[32,256,128]{2,1,0:T(8,128)}), f32[32,256,128]{2,1,0:T(8,128)}, u32[]{:S(2)}, u32[]{:S(2)}) %all-to-all-start.2) | async-done | bytes 4194336 | tf_op jit(solution)/shard_map/all_to_all | solution.py:99
  227.7 4.3 %convolution_divide_fusion = f32[16,128]{1,0:T(8,128)} fusion(f32[8192,128]{1,0:T(8,128)} %bitcast.22, f32[8192]{0:T(1024)S(1)} %bitcast.66, f32[16]{0:T(128)S(1)} %iota_add_fusion, f32[16]{0:T(128)S(1)} %broadcast_maximum_fusion), kind=kOutput, calls=%fused_computation.52 | convolution fusion | flops 201459712 | bytes 4235392 | tf_op jit(solution)/shard_map/dot_general | solution.py:104
  (24 shorter events, 0.2 us)
Async XLA Ops:
  0.6 15.8 %copy-start.6 = (s32[2]{0:T(128)S(1)}, s32[2]{0:T(128)}, u32[]{:S(2)}) copy-start(s32[2]{0:T(128)} %constant.79) | copy-start | bytes 28
  0.6 15.9 %copy-start.5 = (s32[2]{0:T(128)S(1)}, s32[2]{0:T(128)}, u32[]{:S(2)}) copy-start(s32[2]{0:T(128)} %constant.82) | copy-start | bytes 28
  0.7 5.8 %copy-start.1 = (s32[2048,1]{0,1:T(1,128)S(1)}, s32[2048,1]{0,1:T(1,128)}, u32[]{:S(2)}) copy-start(s32[2048,1]{0,1:T(1,128)} %param.6) | copy-start | bytes 24580
  0.7 16.0 %copy-start.3 = (s32[2048]{0:T(1024)S(1)}, s32[2048]{0:T(1024)}, u32[]{:S(2)}) copy-start(s32[2048]{0:T(1024)} %param.7) | copy-start | bytes 24580
  0.7 24.6 %all-to-all-start = ((f32[128,8,256]{2,1,0:T(8,128)}), f32[128,8,256]{2,1,0:T(8,128)S(1)}, u32[]{:S(2)}, u32[]{:S(2)}) async-start(f32[128,8,256]{2,1,0:T(8,128)} %param.5), calls=%async_computation | async-start | bytes 2097152 | tf_op jit(solution)/shard_map/all_to_all | solution.py:73
  15.5 26.8 %copy-start.2 = (s32[2048]{0:T(1024)S(1)}, s32[2048]{0:T(1024)}, u32[]{:S(2)}) copy-start(s32[2048]{0:T(1024)} %param.9) | copy-start | bytes 24580
  16.3 33.9 %copy-start.4 = (s32[2048]{0:T(1024)S(1)}, s32[2048]{0:T(1024)}, u32[]{:S(2)}) copy-start(s32[2048]{0:T(1024)} %param.8) | copy-start | bytes 24580
  25.3 91.0 %all-to-all-start.1 = ((f32[32,1,256]{2,1,0:T(1,128)}), f32[32,1,256]{2,1,0:T(1,128)S(1)}, u32[]{:S(2)}, u32[]{:S(2)}) async-start(f32[32,1,256]{2,1,0:T(1,128)} %bitcast.18), calls=%async_computation.1 | async-start | bytes 65536 | tf_op jit(solution)/shard_map/all_to_all | solution.py:100
  36.5 6.2 %collective-permute-start = (f32[1,64,256]{2,1,0:T(8,128)S(1)}, f32[1,64,256]{2,1,0:T(8,128)S(1)}, u32[]{:S(2)}, u32[]{:S(2)}) collective-permute-start(f32[1,64,256]{2,1,0:T(8,128)S(1)} %get-tuple-element.13), channel_id=1, source_target_pairs={{0,32},{32,64},{64,96},{96,128},{128,160},{160,192},{192,224},{1,3... | collective-permute-start | bytes 196616 | tf_op jit(solution)/shard_map/ppermute | solution.py:15
  39.2 8.3 %collective-permute-start.1 = (f32[1,64,256]{2,1,0:T(8,128)S(1)}, f32[1,64,256]{2,1,0:T(8,128)S(1)}, u32[]{:S(2)}, u32[]{:S(2)}) collective-permute-start(f32[1,64,256]{2,1,0:T(8,128)S(1)} %get-tuple-element.14), channel_id=1, source_target_pairs={{32,0},{64,32},{96,64},{128,96},{160,128},{192,160},{224,192},{33,... | collective-permute-start | bytes 196616 | tf_op jit(solution)/shard_map/ppermute | solution.py:18
  47.5 2.6 %collective-permute-start.2 = (f32[18,1,256]{2,1,0:T(1,128)S(1)}, f32[18,1,256]{2,1,0:T(1,128)S(1)}, u32[]{:S(2)}, u32[]{:S(2)}) collective-permute-start(f32[18,1,256]{2,1,0:T(1,128)S(1)} %get-tuple-element.11), channel_id=1, source_target_pairs={{0,1},{1,2},{2,3},{3,4},{4,5},{5,6},{6,7},{7,8},{8,9},{9,10},{10,1... | collective-permute-start | bytes 55304 | tf_op jit(solution)/shard_map/ppermute | solution.py:15
  48.8 5.1 %collective-permute-start.3 = (f32[18,1,256]{2,1,0:T(1,128)S(1)}, f32[18,1,256]{2,1,0:T(1,128)S(1)}, u32[]{:S(2)}, u32[]{:S(2)}) collective-permute-start(f32[18,1,256]{2,1,0:T(1,128)S(1)} %get-tuple-element.10), channel_id=1, source_target_pairs={{1,0},{2,1},{3,2},{4,3},{5,4},{6,5},{7,6},{8,7},{9,8},{10,9},{11,1... | collective-permute-start | bytes 55304 | tf_op jit(solution)/shard_map/ppermute | solution.py:18
  54.9 12.4 %collective-permute-start.4 = (f32[3,2,64,256]{3,2,1,0:T(8,128)S(1)}, f32[3,2,64,256]{3,2,1,0:T(8,128)S(1)}, u32[]{:S(2)}, u32[]{:S(2)}) collective-permute-start(f32[3,2,64,256]{3,2,1,0:T(8,128)S(1)} %get-tuple-element.4), channel_id=1, source_target_pairs={{0,32},{32,64},{64,96},{96,128},{128,160},{160,192},{192,224},{1,3... | collective-permute-start | bytes 1179656 | tf_op jit(solution)/shard_map/ppermute | solution.py:15
  56.8 14.5 %collective-permute-start.5 = (f32[3,2,64,256]{3,2,1,0:T(8,128)S(1)}, f32[3,2,64,256]{3,2,1,0:T(8,128)S(1)}, u32[]{:S(2)}, u32[]{:S(2)}) collective-permute-start(f32[3,2,64,256]{3,2,1,0:T(8,128)S(1)} %get-tuple-element.5), channel_id=1, source_target_pairs={{32,0},{64,32},{96,64},{128,96},{160,128},{192,160},{224,192},{33,... | collective-permute-start | bytes 1179656 | tf_op jit(solution)/shard_map/ppermute | solution.py:18
  71.4 5.0 %collective-permute-start.6 = (f32[3,20,2,256]{3,2,1,0:T(2,128)S(1)}, f32[3,20,2,256]{3,2,1,0:T(2,128)S(1)}, u32[]{:S(2)}, u32[]{:S(2)}) collective-permute-start(f32[3,20,2,256]{3,2,1,0:T(2,128)S(1)} %get-tuple-element.2), channel_id=1, source_target_pairs={{0,1},{1,2},{2,3},{3,4},{4,5},{5,6},{6,7},{7,8},{8,9},{9,10},{10,1... | collective-permute-start | bytes 368648 | tf_op jit(solution)/shard_map/ppermute | solution.py:15
  74.7 4.8 %collective-permute-start.7 = (f32[3,20,2,256]{3,2,1,0:T(2,128)S(1)}, f32[3,20,2,256]{3,2,1,0:T(2,128)S(1)}, u32[]{:S(2)}, u32[]{:S(2)}) collective-permute-start(f32[3,20,2,256]{3,2,1,0:T(2,128)S(1)} %get-tuple-element.3), channel_id=1, source_target_pairs={{1,0},{2,1},{3,2},{4,3},{5,4},{6,5},{7,6},{8,7},{9,8},{10,9},{11,1... | collective-permute-start | bytes 368648 | tf_op jit(solution)/shard_map/ppermute | solution.py:18
  92.9 6.7 %copy-start = (f32[16,64,256]{2,1,0:T(8,128)}, f32[16,64,256]{2,1,0:T(8,128)S(1)}, u32[]{:S(2)}) copy-start(f32[16,64,256]{2,1,0:T(8,128)S(1)} %fusion.33) | copy-start | bytes 3145732
  116.3 111.4 %all-to-all-start.2 = ((f32[32,256,128]{2,1,0:T(8,128)}), f32[32,256,128]{2,1,0:T(8,128)}, u32[]{:S(2)}, u32[]{:S(2)}) async-start(f32[32,256,128]{2,1,0:T(8,128)} %bitcast.62), calls=%async_computation.2 | async-start | bytes 8388608 | tf_op jit(solution)/shard_map/all_to_all | solution.py:99
where the time goes:
time: 232 us
  waiting for transfers between devices  118 us (51%)
  starting transfers between devices  50.5 us (22%)
  other arithmetic  37.7 us (16%)
  local copies, waits for them, and re-layouts  20.1 us (9%)
  matrix products  4.29 us (2%)
    all_to_all x1, waiting for transfers between devices, local(): lax.all_to_all(buffer, 'bulk', split_axis=0, concat_axis=0, tiled=True)  96.4 us
    ppermute x4, waiting for transfers between devices, padded_2(): lax.ppermute(lax.slice_in_dim(block, 0, width, axis=dim), axis, backward)  15.8 us
    all_to_all x1, starting transfers between devices, local(): lax.all_to_all(buffer, 'bulk', split_axis=0, concat_axis=0, tiled=True)  14.7 us
    all_to_all x1, starting transfers between devices, local(): lax.all_to_all(labels, 'bulk', split_axis=0, concat_axis=0, tiled=True)  11 us
    ppermute x4, starting transfers between devices, padded_2(): lax.ppermute(lax.slice_in_dim(block, 0, width, axis=dim), axis, backward)  9.76 us
    another operation x3, other arithmetic  9.41 us
    ppermute x4, starting transfers between devices, padded_2(): lax.ppermute(lax.slice_in_dim(block, block.shape[dim] - width, None, axis...  9.24 us
    unnamed x4, other arithmetic  9.14 us
  transfers between devices with their start and end apart: 11, of which 7 were waited for; matrix products, arithmetic and copies ran while one was open for 25% of the time, Pallas kernels for 0%

commit v1 on v0

--- a/solution.py
+++ b/solution.py
@@ -5,6 +5,12 @@
 
 PATCH = 128
 F_DEV = 16
+
+
+def swap_blocks(x, name, split, join):
+    parts = jnp.split(x, lax.axis_size(name), axis=split)
+    received = lax.all_to_all(jnp.stack(parts), name, 0, 0)
+    return jnp.concatenate(received, axis=join)
 
 
 def padded_2(block, sides, width):
@@ -70,7 +76,7 @@
 
 
 def local(amp_traces, patch_owner, patch_fault, patch_trace, patch_offset):
-    bricked = lax.all_to_all(amp_traces, "brick", split_axis=0, concat_axis=1, tiled=True)
+    bricked = swap_blocks(amp_traces, "brick", 0, 1)
     near_amp = padded_2(bricked, (("brick", 0), ("bulk", 1)), 1)
     energy = gradient_energy(near_amp)
     rimmed = padded_2(energy, (("brick", 1), ("bulk", 2)), 2)

time: 232 us -> 245 us (1.056)
  local copies, waits for them, and re-layouts: 20.1 us -> 32.6 us
    unnamed x15 -> x22, local copies, waits for them, and re-layouts: 8.66 us -> 19.6 us
  transfers between devices with their start and end apart: 11 -> 11, of which waited for: 7 -> 7; matrix products, arithmetic and copies ran while one was open for 25% -> 24% of each run, Pallas kernels for 0% -> 0%
where the time goes in v1:
time: 245 us; the launch traced here: 244 us
  waiting for transfers between devices  118 us (48%)
  starting transfers between devices  50.5 us (21%)
  other arithmetic  37.7 us (15%)
  local copies, waits for them, and re-layouts  32.6 us (13%)
  matrix products  4.29 us (2%)
    all_to_all x1, waiting for transfers between devices, local(): lax.all_to_all(buffer, 'bulk', split_axis=0, concat_axis=0, tiled=True)  96.4 us
    unnamed x22, local copies, waits for them, and re-layouts  19.6 us
    ppermute x4, waiting for transfers between devices, padded_2(): lax.ppermute(lax.slice_in_dim(block, 0, width, axis=dim), axis, backward)  15.8 us
    all_to_all x1, starting transfers between devices, local(): lax.all_to_all(buffer, 'bulk', split_axis=0, concat_axis=0, tiled=True)  14.7 us
    all_to_all x1, starting transfers between devices, local(): lax.all_to_all(labels, 'bulk', split_axis=0, concat_axis=0, tiled=True)  11 us
    ppermute x4, starting transfers between devices, padded_2(): lax.ppermute(lax.slice_in_dim(block, 0, width, axis=dim), axis, backward)  9.76 us
    another operation x3, other arithmetic  9.41 us
    ppermute x4, starting transfers between devices, padded_2(): lax.ppermute(lax.slice_in_dim(block, block.shape[dim] - width, None, axis...  9.24 us
  transfers between devices with their start and end apart: 11, of which 7 were waited for; matrix products, arithmetic and copies ran while one was open for 24% of the time, Pallas kernels for 0%

profile of v1, /device:TPU:24, one launch (start us, length us, event | category | flops | bytes accessed | tf_op | source)
XLA Modules:
  0.0 244.4 jit_solution(13007489855071283985)
XLA Ops:
  0.6 1.6 bitcast_dynamic-update-slice_fusion.7
  2.2 1.6 bitcast_dynamic-update-slice_fusion.6
  3.8 1.6 bitcast_dynamic-update-slice_fusion.5
  5.3 1.6 bitcast_dynamic-update-slice_fusion.4
  6.9 1.6 bitcast_dynamic-update-slice_fusion.3
  8.5 1.6 bitcast_dynamic-update-slice_fusion.2
  10.0 1.6 bitcast_dynamic-update-slice_fusion.1
  11.6 1.6 bitcast_dynamic-update-slice_fusion
  13.2 5.8 %all-to-all-start = ((f32[8,16,8,256]{3,2,1,0:T(8,128)}), f32[8,16,8,256]{3,2,1,0:T(8,128)S(1)}, u32[]{:S(2)}, u32[]{:S(2)}) async-start(f32[8,16,8,256]{3,2,1,0:T(8,128)} %bitcast_dynamic-update-slice_fusion), calls=%async_computation | async-start | bytes 2097152 | tf_op jit(solution)/shard_map/all_to_all | solution.py:12
  19.0 9.1 %reduce-window.6 = s32[32,16,128]{2,1,0:T(8,128)S(1)} reduce-window(s32[32,16,128]{2,1,0:T(8,128)S(1)} %fusion.51, s32[]{:T(128)} %constant.22.clone.1), window={size=1x1x128 pad=0_0x0_0x127_0}, to_apply=%region_0.1 | reduce-window | flops 8323072 | bytes 524292 | tf_op jit(solution)/shard_map/reduce-window
  28.1 0.1 slice.326
  28.2 0.2 copy.14
  28.4 0.2 reduce-window.9
  28.6 0.1 broadcast_add_fusion
  28.8 0.1 fusion.48
  29.0 0.1 multiply_reduce_fusion
  29.1 0.1 and_reduce_fusion
  29.2 8.6 %scatter_custom_fusion = f32[8192]{0:T(1024)} fusion(s32[2048]{0:T(1024)S(1)} %broadcast_select_fusion, f32[2048]{0:T(1024)S(1)} %convert_add_fusion, f32[]{:T(128)} %constant.18.clone.1), kind=kCustom, calls=%fused_computation.146 | custom fusion | bytes 32772
  37.8 11.0 %all-to-all-start.1 = ((f32[32,1,256]{2,1,0:T(1,128)}), f32[32,1,256]{2,1,0:T(1,128)S(1)}, u32[]{:S(2)}, u32[]{:S(2)}) async-start(f32[32,1,256]{2,1,0:T(1,128)} %bitcast.24), calls=%async_computation.1 | async-start | bytes 65536 | tf_op jit(solution)/shard_map/all_to_all | solution.py:106
  48.9 2.8 %collective-permute-start = (f32[1,64,256]{2,1,0:T(8,128)S(1)}, f32[1,64,256]{2,1,0:T(8,128)S(1)}, u32[]{:S(2)}, u32[]{:S(2)}) collective-permute-start(f32[1,64,256]{2,1,0:T(8,128)S(1)} %get-tuple-element.13), channel_id=1, source_target_pairs={{0,32},{32,64},{64,96},{96,128},{128,160},{160,192},{192,224},{1,3... | collective-permute-start | bytes 196616 | tf_op jit(solution)/shard_map/ppermute | solution.py:21
  51.7 3.1 %collective-permute-start.1 = (f32[1,64,256]{2,1,0:T(8,128)S(1)}, f32[1,64,256]{2,1,0:T(8,128)S(1)}, u32[]{:S(2)}, u32[]{:S(2)}) collective-permute-start(f32[1,64,256]{2,1,0:T(8,128)S(1)} %get-tuple-element.14), channel_id=1, source_target_pairs={{32,0},{64,32},{96,64},{128,96},{160,128},{192,160},{224,192},{33,... | collective-permute-start | bytes 196616 | tf_op jit(solution)/shard_map/ppermute | solution.py:24
  54.8 0.1 copy_bitcast_fusion
  54.9 0.2 collective-permute-done
  55.1 4.9 %collective-permute-done.1 = f32[1,64,256]{2,1,0:T(8,128)S(1)} collective-permute-done((f32[1,64,256]{2,1,0:T(8,128)S(1)}, f32[1,64,256]{2,1,0:T(8,128)S(1)}, u32[]{:S(2)}, u32[]{:S(2)}) %collective-permute-start.1) | collective-permute-done | bytes 65568 | tf_op jit(solution)/shard_map/ppermute | solution.py:24
  60.0 1.3 collective-permute-start.2
  61.3 1.3 collective-permute-start.3
  62.6 3.8 %collective-permute-done.3 = f32[18,1,256]{2,1,0:T(1,128)S(1)} collective-permute-done((f32[18,1,256]{2,1,0:T(1,128)S(1)}, f32[18,1,256]{2,1,0:T(1,128)S(1)}, u32[]{:S(2)}, u32[]{:S(2)}) %collective-permute-start.3) | collective-permute-done | bytes 18464 | tf_op jit(solution)/shard_map/ppermute | solution.py:24
  66.4 0.9 fusion.42
  67.4 1.9 collective-permute-start.4
  69.3 3.9 %collective-permute-start.5 = (f32[3,2,64,256]{3,2,1,0:T(8,128)S(1)}, f32[3,2,64,256]{3,2,1,0:T(8,128)S(1)}, u32[]{:S(2)}, u32[]{:S(2)}) collective-permute-start(f32[3,2,64,256]{3,2,1,0:T(8,128)S(1)} %get-tuple-element.5), channel_id=1, source_target_pairs={{32,0},{64,32},{96,64},{128,96},{160,128},{192,160},{224,192},{33,... | collective-permute-start | bytes 1179656 | tf_op jit(solution)/shard_map/ppermute | solution.py:24
  73.2 0.2 pad_maximum_fusion.1
  73.4 0.2 slice_add_fusion.8
  73.6 0.2 fusion.43
  73.9 5.9 %collective-permute-done.4 = f32[3,2,64,256]{3,2,1,0:T(8,128)S(1)} collective-permute-done((f32[3,2,64,256]{3,2,1,0:T(8,128)S(1)}, f32[3,2,64,256]{3,2,1,0:T(8,128)S(1)}, u32[]{:S(2)}, u32[]{:S(2)}) %collective-permute-start.4) | collective-permute-done | bytes 393248 | tf_op jit(solution)/shard_map/ppermute | solution.py:21
  79.7 4.0 %collective-permute-done.5 = f32[3,2,64,256]{3,2,1,0:T(8,128)S(1)} collective-permute-done((f32[3,2,64,256]{3,2,1,0:T(8,128)S(1)}, f32[3,2,64,256]{3,2,1,0:T(8,128)S(1)}, u32[]{:S(2)}, u32[]{:S(2)}) %collective-permute-start.5) | collective-permute-done | bytes 393248 | tf_op jit(solution)/shard_map/ppermute | solution.py:24
  83.8 3.3 %collective-permute-start.6 = (f32[3,20,2,256]{3,2,1,0:T(2,128)S(1)}, f32[3,20,2,256]{3,2,1,0:T(2,128)S(1)}, u32[]{:S(2)}, u32[]{:S(2)}) collective-permute-start(f32[3,20,2,256]{3,2,1,0:T(2,128)S(1)} %get-tuple-element.2), channel_id=1, source_target_pairs={{0,1},{1,2},{2,3},{3,4},{4,5},{5,6},{6,7},{7,8},{8,9},{9,10},{10,1... | collective-permute-start | bytes 368648 | tf_op jit(solution)/shard_map/ppermute | solution.py:21
  87.1 1.5 collective-permute-start.7
  88.6 0.2 slice_add_fusion.13
  88.8 3.1 %collective-permute-done.7 = f32[3,20,2,256]{3,2,1,0:T(2,128)S(1)} collective-permute-done((f32[3,20,2,256]{3,2,1,0:T(2,128)S(1)}, f32[3,20,2,256]{3,2,1,0:T(2,128)S(1)}, u32[]{:S(2)}, u32[]{:S(2)}) %collective-permute-start.7) | collective-permute-done | bytes 122912 | tf_op jit(solution)/shard_map/ppermute | solution.py:24
  92.0 0.9 pad_maximum_fusion
  92.9 0.5 slice_add_fusion
  93.3 1.2 slice_add_fusion.4
  94.6 4.9 %fusion.3 = f32[3,16,64,256]{3,2,1,0:T(8,128)} fusion(f32[3,16,64,256]{3,2,1,0:T(8,128)S(1)} %slice_add_fusion.4), kind=kLoop, calls=%fused_computation.15 | loop fusion | flops 3145728 | bytes 6291456 | tf_op jit(solution)/shard_map/add | solution.py:33
  99.5 5.9 %fusion.33 = f32[16,64,256]{2,1,0:T(8,128)S(1)} fusion(f32[3,16,64,256]{3,2,1,0:T(8,128)} %fusion.3, f32[16,64,256]{2,1,0:T(8,128)S(1)} %slice_add_fusion.13, f32[16,64,256]{2,1,0:T(8,128)S(1)} %fusion.43), kind=kLoop, calls=%fused_computation.82 | loop fusion | flops 6553600 | bytes 6291456 | tf_op jit(solution)/shard_map/mul | solution.py:61
  105.4 6.6 %gather_fusion = f32[2048,256]{1,0:T(8,128)S(1)} fusion(f32[1024,256]{1,0:T(8,128)S(1)} %bitcast.71, s32[2048]{0:T(1024)S(1)} %fusion.54), kind=kCustom, calls=%fused_computation | custom fusion | bytes 4202496 | tf_op jit(solution)/shard_map/gather | solution.py:85
  112.1 0.6 slice.328
  112.7 0.5 pad_select_fusion.6
  113.2 0.6 slice.329
  113.8 0.4 pad_select_fusion.5
  114.2 0.6 slice.330
  114.8 0.4 pad_select_fusion.4
  115.3 0.6 slice.331
  115.9 0.4 pad_select_fusion.3
  116.4 0.6 slice.332
  117.0 0.7 pad_select_fusion.2
  117.6 0.6 slice.333
  118.2 0.4 pad_select_fusion.1
  118.7 0.6 slice.334
  119.3 0.4 pad_select_fusion
  119.8 8.9 %scatter_custom_fusion.1 = f32[8192,128]{1,0:T(8,128)} fusion(s32[2048]{0:T(1024)S(1)} %broadcast_select_fusion, f32[]{:T(128)} %constant.18.clone.1, f32[2048,256]{1,0:T(8,128)S(1)} %pad_select_fusion, f32[2048,128]{1,0:T(8,128)S(1)} %slice.335, pred[2048]{0:T(1024)(128)(4,1)S(1)} %get-tuple-element.15), kind=kCustom, calls=%fused_computation.36 | custom fusion | flops 262144 | bytes 6294528
  128.8 14.7 %all-to-all-start.2 = ((f32[32,256,128]{2,1,0:T(8,128)}), f32[32,256,128]{2,1,0:T(8,128)}, u32[]{:S(2)}, u32[]{:S(2)}) async-start(f32[32,256,128]{2,1,0:T(8,128)} %bitcast.72), calls=%async_computation.2 | async-start | bytes 8388608 | tf_op jit(solution)/shard_map/all_to_all | solution.py:105
  143.5 0.3 fusion.45
  143.7 96.4 %all-to-all-done.2 = f32[32,256,128]{2,1,0:T(8,128)} async-done(((f32[32,256,128]{2,1,0:T(8,128)}), f32[32,256,128]{2,1,0:T(8,128)}, u32[]{:S(2)}, u32[]{:S(2)}) %all-to-all-start.2) | async-done | bytes 4194336 | tf_op jit(solution)/shard_map/all_to_all | solution.py:105
  240.1 4.3 %convolution_divide_fusion = f32[16,128]{1,0:T(8,128)} fusion(f32[8192,128]{1,0:T(8,128)} %bitcast.28, f32[8192]{0:T(1024)S(1)} %bitcast.76, f32[16]{0:T(128)S(1)} %iota_add_fusion, f32[16]{0:T(128)S(1)} %broadcast_maximum_fusion), kind=kOutput, calls=%fused_computation.52 | convolution fusion | flops 201459712 | bytes 4235392 | tf_op jit(solution)/shard_map/dot_general | solution.py:110
  (32 shorter events, 0.4 us)
Async XLA Ops:
  0.6 18.3 %copy-start.1 = (s32[2048,1]{0,1:T(1,128)S(1)}, s32[2048,1]{0,1:T(1,128)}, u32[]{:S(2)}) copy-start(s32[2048,1]{0,1:T(1,128)} %param.6) | copy-start | bytes 24580
  13.2 15.8 %copy-start.6 = (s32[2]{0:T(128)S(1)}, s32[2]{0:T(128)}, u32[]{:S(2)}) copy-start(s32[2]{0:T(128)} %constant.79) | copy-start | bytes 28
  13.2 15.9 %copy-start.5 = (s32[2]{0:T(128)S(1)}, s32[2]{0:T(128)}, u32[]{:S(2)}) copy-start(s32[2]{0:T(128)} %constant.82) | copy-start | bytes 28
  13.2 16.0 %copy-start.3 = (s32[2048]{0:T(1024)S(1)}, s32[2048]{0:T(1024)}, u32[]{:S(2)}) copy-start(s32[2048]{0:T(1024)} %param.7) | copy-start | bytes 24580
  13.2 24.6 %copy-start.2 = (s32[2048]{0:T(1024)S(1)}, s32[2048]{0:T(1024)}, u32[]{:S(2)}) copy-start(s32[2048]{0:T(1024)} %param.9) | copy-start | bytes 24580
  13.2 24.6 %all-to-all-start = ((f32[8,16,8,256]{3,2,1,0:T(8,128)}), f32[8,16,8,256]{3,2,1,0:T(8,128)S(1)}, u32[]{:S(2)}, u32[]{:S(2)}) async-start(f32[8,16,8,256]{3,2,1,0:T(8,128)} %bitcast_dynamic-update-slice_fusion), calls=%async_computation | async-start | bytes 2097152 | tf_op jit(solution)/shard_map/all_to_all | solution.py:12
  28.8 33.8 %copy-start.4 = (s32[2048]{0:T(1024)S(1)}, s32[2048]{0:T(1024)}, u32[]{:S(2)}) copy-start(s32[2048]{0:T(1024)} %param.8) | copy-start | bytes 24580
  37.8 90.9 %all-to-all-start.1 = ((f32[32,1,256]{2,1,0:T(1,128)}), f32[32,1,256]{2,1,0:T(1,128)S(1)}, u32[]{:S(2)}, u32[]{:S(2)}) async-start(f32[32,1,256]{2,1,0:T(1,128)} %bitcast.24), calls=%async_computation.1 | async-start | bytes 65536 | tf_op jit(solution)/shard_map/all_to_all | solution.py:106
  48.9 6.2 %collective-permute-start = (f32[1,64,256]{2,1,0:T(8,128)S(1)}, f32[1,64,256]{2,1,0:T(8,128)S(1)}, u32[]{:S(2)}, u32[]{:S(2)}) collective-permute-start(f32[1,64,256]{2,1,0:T(8,128)S(1)} %get-tuple-element.13), channel_id=1, source_target_pairs={{0,32},{32,64},{64,96},{96,128},{128,160},{160,192},{192,224},{1,3... | collective-permute-start | bytes 196616 | tf_op jit(solution)/shard_map/ppermute | solution.py:21
  51.7 8.3 %collective-permute-start.1 = (f32[1,64,256]{2,1,0:T(8,128)S(1)}, f32[1,64,256]{2,1,0:T(8,128)S(1)}, u32[]{:S(2)}, u32[]{:S(2)}) collective-permute-start(f32[1,64,256]{2,1,0:T(8,128)S(1)} %get-tuple-element.14), channel_id=1, source_target_pairs={{32,0},{64,32},{96,64},{128,96},{160,128},{192,160},{224,192},{33,... | collective-permute-start | bytes 196616 | tf_op jit(solution)/shard_map/ppermute | solution.py:24
  60.0 2.6 %collective-permute-start.2 = (f32[18,1,256]{2,1,0:T(1,128)S(1)}, f32[18,1,256]{2,1,0:T(1,128)S(1)}, u32[]{:S(2)}, u32[]{:S(2)}) collective-permute-start(f32[18,1,256]{2,1,0:T(1,128)S(1)} %get-tuple-element.11), channel_id=1, source_target_pairs={{0,1},{1,2},{2,3},{3,4},{4,5},{5,6},{6,7},{7,8},{8,9},{9,10},{10,1... | collective-permute-start | bytes 55304 | tf_op jit(solution)/shard_map/ppermute | solution.py:21
  61.3 5.1 %collective-permute-start.3 = (f32[18,1,256]{2,1,0:T(1,128)S(1)}, f32[18,1,256]{2,1,0:T(1,128)S(1)}, u32[]{:S(2)}, u32[]{:S(2)}) collective-permute-start(f32[18,1,256]{2,1,0:T(1,128)S(1)} %get-tuple-element.10), channel_id=1, source_target_pairs={{1,0},{2,1},{3,2},{4,3},{5,4},{6,5},{7,6},{8,7},{9,8},{10,9},{11,1... | collective-permute-start | bytes 55304 | tf_op jit(solution)/shard_map/ppermute | solution.py:24
  67.4 12.4 %collective-permute-start.4 = (f32[3,2,64,256]{3,2,1,0:T(8,128)S(1)}, f32[3,2,64,256]{3,2,1,0:T(8,128)S(1)}, u32[]{:S(2)}, u32[]{:S(2)}) collective-permute-start(f32[3,2,64,256]{3,2,1,0:T(8,128)S(1)} %get-tuple-element.4), channel_id=1, source_target_pairs={{0,32},{32,64},{64,96},{96,128},{128,160},{160,192},{192,224},{1,3... | collective-permute-start | bytes 1179656 | tf_op jit(solution)/shard_map/ppermute | solution.py:21
  69.3 14.5 %collective-permute-start.5 = (f32[3,2,64,256]{3,2,1,0:T(8,128)S(1)}, f32[3,2,64,256]{3,2,1,0:T(8,128)S(1)}, u32[]{:S(2)}, u32[]{:S(2)}) collective-permute-start(f32[3,2,64,256]{3,2,1,0:T(8,128)S(1)} %get-tuple-element.5), channel_id=1, source_target_pairs={{32,0},{64,32},{96,64},{128,96},{160,128},{192,160},{224,192},{33,... | collective-permute-start | bytes 1179656 | tf_op jit(solution)/shard_map/ppermute | solution.py:24
  83.8 5.0 %collective-permute-start.6 = (f32[3,20,2,256]{3,2,1,0:T(2,128)S(1)}, f32[3,20,2,256]{3,2,1,0:T(2,128)S(1)}, u32[]{:S(2)}, u32[]{:S(2)}) collective-permute-start(f32[3,20,2,256]{3,2,1,0:T(2,128)S(1)} %get-tuple-element.2), channel_id=1, source_target_pairs={{0,1},{1,2},{2,3},{3,4},{4,5},{5,6},{6,7},{7,8},{8,9},{9,10},{10,1... | collective-permute-start | bytes 368648 | tf_op jit(solution)/shard_map/ppermute | solution.py:21
  87.1 4.8 %collective-permute-start.7 = (f32[3,20,2,256]{3,2,1,0:T(2,128)S(1)}, f32[3,20,2,256]{3,2,1,0:T(2,128)S(1)}, u32[]{:S(2)}, u32[]{:S(2)}) collective-permute-start(f32[3,20,2,256]{3,2,1,0:T(2,128)S(1)} %get-tuple-element.3), channel_id=1, source_target_pairs={{1,0},{2,1},{3,2},{4,3},{5,4},{6,5},{7,6},{8,7},{9,8},{10,9},{11,1... | collective-permute-start | bytes 368648 | tf_op jit(solution)/shard_map/ppermute | solution.py:24
  105.4 6.7 %copy-start = (f32[16,64,256]{2,1,0:T(8,128)}, f32[16,64,256]{2,1,0:T(8,128)S(1)}, u32[]{:S(2)}) copy-start(f32[16,64,256]{2,1,0:T(8,128)S(1)} %fusion.33) | copy-start | bytes 3145732
  128.8 111.4 %all-to-all-start.2 = ((f32[32,256,128]{2,1,0:T(8,128)}), f32[32,256,128]{2,1,0:T(8,128)}, u32[]{:S(2)}, u32[]{:S(2)}) async-start(f32[32,256,128]{2,1,0:T(8,128)} %bitcast.72), calls=%async_computation.2 | async-start | bytes 8388608 | tf_op jit(solution)/shard_map/all_to_all | solution.py:105
